TPU v7x, 32 devices: a whole 2x2x4 slice. The times are simulated.
32 devices in a mesh: rep: 2 (over x), shard: 16 (over z, y, core).
Axes of the slice: x: 2, y: 2, z: 4, core: 2. Of those that a mesh axis runs over, the one named last changes fastest.
Arguments:
- tokens: bfloat16 [32, 192, 2048], P(('rep', 'shard')), may hold values from -7 to 7
- segment_ids: int32 [32, 192], P(('rep', 'shard')), may hold values from 0 to 3, never falling along the last dimension, each value on 1 to 96 neighbouring positions
- norm_gain: bfloat16 [2048], P('shard'), may hold values from 0.25 to 1.75
- input_weight: bfloat16 [2048, 2048], P('shard'), may hold values from -0.125 to 0.125
- forget_weight: bfloat16 [2048, 2048], P('shard'), may hold values from -0.5 to 0.5
- gate_weight: bfloat16 [2048, 2048], P('shard'), may hold values from -0.125 to 0.125
- mixer_gain: bfloat16 [2048], P('shard'), may hold values from 0.25 to 1.75
- out_weight: bfloat16 [2048, 2048], P('shard'), may hold values from -0.1875 to 0.1875
- ffn_gain: bfloat16 [2048], P('shard'), may hold values from 0.25 to 1.75
- ffn_gate_weight: bfloat16 [2048, 5632], P('shard'), may hold values from -0.125 to 0.125
- ffn_up_weight: bfloat16 [2048, 5632], P('shard'), may hold values from -0.125 to 0.125
- ffn_down_weight: bfloat16 [5632, 2048], P('shard'), may hold values from -0.15625 to 0.15625
- cotangent: bfloat16 [32, 192, 2048], P(('rep', 'shard')), may hold values from -6 to 6
Outputs:
- block_output: bfloat16 [32, 192, 2048], P(('rep', 'shard'))
- input_grad: bfloat16 [32, 192, 2048], P(('rep', 'shard'))
- norm_gain_grad: float32 [2048], P('shard')
- input_weight_grad: float32 [2048, 2048], P('shard')
- forget_weight_grad: float32 [2048, 2048], P('shard')
- gate_weight_grad: float32 [2048, 2048], P('shard')
- mixer_gain_grad: float32 [2048], P('shard')
- out_weight_grad: float32 [2048, 2048], P('shard')
- ffn_gain_grad: float32 [2048], P('shard')
- ffn_gate_grad: float32 [2048, 5632], P('shard')
- ffn_up_grad: float32 [2048, 5632], P('shard')
- ffn_down_grad: float32 [5632, 2048], P('shard')
Inputs may be any that keep to these rules, and one draw needn't show every extreme that they name: `segment_ids`: document numbers never fall along a sequence; each document has 1 to 96 tokens, and one has exactly 96.
All inputs are finite; a program needn't handle non-finite values.
Results may differ from a plain program's by a relative error of at most 0.019.
Values may be sent and summed in bfloat16 or wider, within the bound.
No kernel may reach another device: no remote copies, remote signals or barrier semaphores. Data moves between devices by JAX's collectives and lax.ppermute only.
A program may use at most 640 MiB of HBM per device.

v0:
```python
import jax
import jax.numpy as jnp
from jax import lax
from jax.sharding import PartitionSpec as P

EPSILON = 1e-06


def normalize(values):
    scale = lax.rsqrt(jnp.mean(values * values, axis=-1, keepdims=True) + EPSILON)
    return (values * scale, scale)


def norm_back(grad_scaled, scaled, scale):
    inner = jnp.mean(grad_scaled * scaled, axis=-1, keepdims=True)
    return scale * (grad_scaled - scaled * inner)


def swish_pair(values):
    sigma = jax.nn.sigmoid(values)
    return (values * sigma, sigma * (1.0 + values * (1.0 - sigma)))


def combine_steps(earlier, later):
    return (earlier[0] * later[0], later[0] * earlier[1] + later[1])


def linear_scan(decay, update):
    return lax.associative_scan(combine_steps, (decay, update), axis=0)[1]


def contract_rows(left, piece):
    return lax.dot_general(
        left, piece, (((1,), (1,)), ((), ())), preferred_element_type=jnp.float32
    )


def gain_folder(scaled, carry, pieces):
    sums, fulls, gain_full = carry
    gain_piece = pieces[-1]
    matrices = pieces[:-1]
    columns = scaled * gain_piece.astype(jnp.float32)
    lowered = columns.astype(jnp.bfloat16)
    sums = tuple(
        (jnp.dot(lowered, piece, preferred_element_type=jnp.float32) for piece in matrices)
    )
    gain_full = gain_piece
    return (sums, fulls, gain_full)


def plain_folder(lowered_rows, carry, piece):
    total, full = carry
    total = jnp.dot(lowered_rows, piece, preferred_element_type=jnp.float32)
    return (total, full)


def start_carry(length, width, columns, number):
    sums = tuple((jnp.zeros((length, columns), jnp.float32) for index in range(number)))
    fulls = ()
    return (sums, fulls, jnp.zeros((width,), jnp.bfloat16))


def single_columns(left, piece):
    return contract_rows(left, piece)


def multi_columns(lefts, pieces):
    total = contract_rows(lefts[0], pieces[0])
    for left, piece in zip(lefts[1:], pieces[1:]):
        total = total + contract_rows(left, piece)
    return total


def row_grad(left, right):
    return lax.dot_general(
        left, right, (((0,), (0,)), ((), ())), preferred_element_type=jnp.float32
    )


def row_block(pairs, gains):
    pieces = [row_grad(left, right) for left, right in pairs]
    pieces = pieces + [vector[:, None] for vector in gains]
    return jnp.concatenate(pieces, axis=1)


def shards(
    tokens,
    segment_ids,
    norm_gain,
    input_weight,
    forget_weight,
    gate_weight,
    mixer_gain,
    out_weight,
    ffn_gain,
    ffn_gate_weight,
    ffn_up_weight,
    ffn_down_weight,
    cotangent,
):
    inputs = tokens[0].astype(jnp.float32)
    length, width = inputs.shape
    hidden_width = ffn_up_weight.shape[1]
    segments = segment_ids[0]
    same = jnp.concatenate(
        [jnp.zeros((1,), jnp.float32), (segments[1:] == segments[:-1]).astype(jnp.float32)]
    )
    scaled_in, scale_in = normalize(inputs)
    mixer_sums, mixer_full, gain_one = gain_folder(
        scaled_in,
        start_carry(length, width, width, 3),
        (
            lax.all_gather(input_weight, "shard", axis=0, tiled=True),
            lax.all_gather(forget_weight, "shard", axis=0, tiled=True),
            lax.all_gather(gate_weight, "shard", axis=0, tiled=True),
            lax.all_gather(norm_gain, "shard", axis=0, tiled=True),
        ),
    )
    input_pre, forget_pre, gate_pre = mixer_sums
    forget = jax.nn.sigmoid(forget_pre)
    input_act, input_slope = swish_pair(input_pre)
    update = input_act * (1.0 - forget)
    decay = forget * same[:, None]
    state = linear_scan(decay, update)
    state_scaled, state_scale = normalize(state)
    gate_act, gate_slope = swish_pair(gate_pre)
    mixed_pre = state_scaled * gate_act
    out_sums, out_full, gain_two = gain_folder(
        mixed_pre,
        start_carry(length, width, width, 1),
        (
            lax.all_gather(out_weight, "shard", axis=0, tiled=True),
            lax.all_gather(mixer_gain, "shard", axis=0, tiled=True),
        ),
    )
    resid = inputs + out_sums[0]
    scaled_mid, scale_mid = normalize(resid)
    ffn_sums, ffn_full, gain_three = gain_folder(
        scaled_mid,
        start_carry(length, width, hidden_width, 2),
        (
            lax.all_gather(ffn_gate_weight, "shard", axis=0, tiled=True),
            lax.all_gather(ffn_up_weight, "shard", axis=0, tiled=True),
            lax.all_gather(ffn_gain, "shard", axis=0, tiled=True),
        ),
    )
    ffn_gate, ffn_up = ffn_sums
    ffn_act, ffn_slope = swish_pair(ffn_gate)
    hidden = (ffn_act * ffn_up).astype(jnp.bfloat16)
    down_start = (jnp.zeros((length, width), jnp.float32), jnp.zeros((1, 1), jnp.bfloat16))
    ffn_out, down_full = plain_folder(
        hidden, down_start, lax.all_gather(ffn_down_weight, "shard", axis=0, tiled=True)
    )
    block_output = (resid + ffn_out).astype(jnp.bfloat16)
    grad_out = cotangent[0]
    grad_hidden = single_columns(
        grad_out, lax.all_gather(ffn_down_weight, "shard", axis=0, tiled=True)
    )
    grad_fgate = (grad_hidden * ffn_up * ffn_slope).astype(jnp.bfloat16)
    grad_fup = (grad_hidden * ffn_act).astype(jnp.bfloat16)
    grad_ffn_in = multi_columns(
        (grad_fgate, grad_fup),
        lax.all_gather((ffn_gate_weight, ffn_up_weight), "shard", axis=0, tiled=True),
    )
    gain_three_f = gain_three.astype(jnp.float32)
    mid_low = (scaled_mid * gain_three_f).astype(jnp.bfloat16)
    gain_three_grad = jnp.sum(grad_ffn_in * scaled_mid, axis=0)
    grad_resid = grad_out.astype(jnp.float32) + norm_back(
        grad_ffn_in * gain_three_f, scaled_mid, scale_mid
    )
    grad_branch = grad_resid.astype(jnp.bfloat16)
    grad_mixed = single_columns(
        grad_branch, lax.all_gather(out_weight, "shard", axis=0, tiled=True)
    )
    gain_two_f = gain_two.astype(jnp.float32)
    mixed_low = (mixed_pre * gain_two_f).astype(jnp.bfloat16)
    gain_two_grad = jnp.sum(grad_mixed * mixed_pre, axis=0)
    weighted = grad_mixed * gain_two_f
    grad_gate_pre = (weighted * state_scaled * gate_slope).astype(jnp.bfloat16)
    grad_state = norm_back(weighted * gate_act, state_scaled, state_scale)
    next_decay = jnp.concatenate([decay[1:], jnp.zeros((1, width), jnp.float32)])
    carried = jnp.flip(linear_scan(jnp.flip(next_decay, 0), jnp.flip(grad_state, 0)), 0)
    previous = jnp.concatenate([jnp.zeros((1, width), jnp.float32), state[:-1]])
    grad_forget = carried * previous * same[:, None] - carried * input_act
    grad_input_pre = (carried * (1.0 - forget) * input_slope).astype(jnp.bfloat16)
    grad_forget_pre = (grad_forget * forget * (1.0 - forget)).astype(jnp.bfloat16)
    triple = (grad_input_pre, grad_forget_pre, grad_gate_pre)
    grad_normed = multi_columns(
        triple,
        lax.all_gather((input_weight, forget_weight, gate_weight), "shard", axis=0, tiled=True),
    )
    gain_one_f = gain_one.astype(jnp.float32)
    in_low = (scaled_in * gain_one_f).astype(jnp.bfloat16)
    gain_one_grad = jnp.sum(grad_normed * scaled_in, axis=0)
    input_grad = (grad_resid + norm_back(grad_normed * gain_one_f, scaled_in, scale_in)).astype(
        jnp.bfloat16
    )
    triple_joined = jnp.concatenate(triple, axis=1)
    pair_joined = jnp.concatenate([grad_fgate, grad_fup], axis=1)
    pairs = ((in_low, triple_joined), (mixed_low, grad_branch), (mid_low, pair_joined))
    gains = (gain_one_grad, gain_two_grad, gain_three_grad)
    rows_term = lax.psum_scatter(
        row_block(pairs, gains).astype(jnp.bfloat16), "shard", scatter_dimension=0, tiled=True
    )
    down_term = lax.psum_scatter(
        row_grad(hidden, grad_out).astype(jnp.bfloat16), "shard", scatter_dimension=0, tiled=True
    )
    rows_total, down_total = (
        lax.psum(rows_term, "rep").astype(jnp.float32),
        lax.psum(down_term, "rep").astype(jnp.float32),
    )
    tail = 4 * width + 2 * hidden_width
    return (
        block_output[None],
        input_grad[None],
        rows_total[:, tail],
        rows_total[:, :width],
        rows_total[:, width : 2 * width],
        rows_total[:, 2 * width : 3 * width],
        rows_total[:, tail + 1],
        rows_total[:, 3 * width : 4 * width],
        rows_total[:, tail + 2],
        rows_total[:, 4 * width : 4 * width + hidden_width],
        rows_total[:, 4 * width + hidden_width : tail],
        down_total,
    )


def solution(mesh):
    placed = (
        P(("rep", "shard"), None, None),
        P(("rep", "shard"), None),
        P("shard"),
        P("shard", None),
        P("shard", None),
        P("shard", None),
        P("shard"),
        P("shard", None),
        P("shard"),
        P("shard", None),
        P("shard", None),
        P("shard", None),
        P(("rep", "shard"), None, None),
    )
    return jax.shard_map(
        shards,
        mesh=mesh,
        in_specs=placed,
        out_specs=(
            P(("rep", "shard"), None, None),
            P(("rep", "shard"), None, None),
            P("shard"),
            P("shard", None),
            P("shard", None),
            P("shard", None),
            P("shard"),
            P("shard", None),
            P("shard"),
            P("shard", None),
            P("shard", None),
            P("shard", None),
        ),
        check_vma=False,
    )
```

profile of v0, /device:TPU:0, one launch (start us, length us, event | category | flops | bytes accessed | tf_op | source)
XLA Modules:
  0.0 2012.6 jit_solution(17651145178794768228)
XLA Ops:
  12.0 23.2 %all-gather = bf16[16,1,128]{2,1,0:T(2,128)(2,1)S(1)} all-gather(bf16[1,1,128]{2,1,0:T(2,128)(2,1)S(1)} %bitcast.75), channel_id=1, replica_groups=mesh['rep'=2,'shard'=16] {'shard'}, dimensions={0}, use_global_device_ids=true | all-gather | bytes 4352 | tf_op jit(solution)/shard_map/all_gather | solution.py:116
  35.2 17.5 all-gather.1
  52.7 18.9 all-gather.2
  72.6 15.3 all-gather.11.cloned.1.call-done
  87.9 6.4 fusion.57
  94.3 69.0 %all-gather.13.cloned.1.call-done = bf16[2048,2048]{1,0:T(8,128)(2,1)} async-done(((bf16[128,2048]{1,0:T(8,128)(2,1)}), bf16[2048,2048]{1,0:T(8,128)(2,1)}) %all-gather.13.cloned.1.call-update) | async-done | bytes 8388624 | tf_op jit(solution)/shard_map/all_gather | solution.py:114
  163.3 7.8 broadcast_multiply_fusion
  177.4 4.4 slice.444
  200.5 38.1 %all-gather.15.cloned.1.call-done = bf16[2048,2048]{1,0:T(8,128)(2,1)} async-done(((bf16[128,2048]{1,0:T(8,128)(2,1)}), bf16[2048,2048]{1,0:T(8,128)(2,1)}) %all-gather.15.cloned.1.call-update) | async-done | bytes 8388624 | tf_op jit(solution)/shard_map/all_gather | solution.py:115
  238.6 7.6 multiply_multiply_fusion.1
  246.2 67.6 %all-gather.17.cloned.1.call-done = bf16[2048,2048]{1,0:T(8,128)(2,1)} async-done(((bf16[128,2048]{1,0:T(8,128)(2,1)}), bf16[2048,2048]{1,0:T(8,128)(2,1)}) %all-gather.17.cloned.1.call-update) | async-done | bytes 8388624 | tf_op jit(solution)/shard_map/all_gather | solution.py:132
  313.8 5.9 multiply_reduce_fusion.4
  322.0 110.3 %all-gather.21.cloned.1.call-done = bf16[2048,5632]{1,0:T(8,128)(2,1)} async-done(((bf16[128,5632]{1,0:T(8,128)(2,1)}), bf16[2048,5632]{1,0:T(8,128)(2,1)}) %all-gather.21.cloned.1.call-update) | async-done | bytes 23068688 | tf_op jit(solution)/shard_map/all_gather | solution.py:143
  432.3 14.5 fusion.74
  446.8 105.7 %all-gather.19.cloned.1.call-done = bf16[2048,5632]{1,0:T(8,128)(2,1)} async-done(((bf16[128,5632]{1,0:T(8,128)(2,1)}), bf16[2048,5632]{1,0:T(8,128)(2,1)}) %all-gather.19.cloned.1.call-update) | async-done | bytes 23068688 | tf_op jit(solution)/shard_map/all_gather | solution.py:142
  552.4 14.7 fusion.73
  567.1 105.7 %all-gather.23.cloned.1.call-done = bf16[5632,2048]{1,0:T(8,128)(2,1)} async-done(((bf16[352,2048]{1,0:T(8,128)(2,1)}), bf16[5632,2048]{1,0:T(8,128)(2,1)}) %all-gather.23.cloned.1.call-update) | async-done | bytes 23068688 | tf_op jit(solution)/shard_map/all_gather | solution.py:152
  672.8 16.0 multiply_convert_fusion
  690.1 10.9 convolution_convert_fusion.1
  703.9 4.4 slice.456
  708.3 4.5 slice.449
  712.8 4.5 slice.447
  717.3 8.6 slice.457
  725.9 8.7 slice.448
  734.6 8.6 slice.450
  745.4 12.1 fusion.75
  757.6 14.4 multiply_reduce_fusion
  775.2 8.6 multiply_reduce_fusion.1
  791.4 8.6 slice.452
  800.1 5.1 slice.454
  824.8 5.5 slice.504
  838.6 5.2 pad.115
  846.6 16.0 rev.6
  862.6 4.1 multiply_convert_fusion.4
  866.8 6.8 fusion.76
  873.7 2.9 convolution_add_fusion.1
  876.7 4.3 fusion.24
  882.1 5.8 convolution_convert_fusion.3
  887.9 12.3 copy.30
  900.2 13.6 convolution_convert_fusion.2
  913.7 20.9 %convolution_convert_fusion = bf16[2048,11264]{1,0:T(8,128)(2,1)} fusion(bf16[192,2048]{1,0:T(8,128)(2,1)} %multiply_convert_fusion.6, bf16[192,5632]{1,0:T(8,128)(2,1)} %get-tuple-element.29, bf16[192,5632]{1,0:T(8,128)(2,1)} %get-tuple-element.30), kind=kOutput, calls=%fused_computation | convolution fusion | flops 8890089472 | bytes 51249152 | tf_op jit(solution)/shard_map/dot_general | solution.py:75
  934.6 158.1 %concatenate.84 = bf16[2048,19459]{1,0:T(8,128)(2,1)} concatenate(bf16[2048,6144]{1,0:T(8,128)(2,1)} %convolution_convert_fusion.2, bf16[2048,2048]{1,0:T(8,128)(2,1)} %copy.30, bf16[2048,11264]{1,0:T(8,128)(2,1)} %convolution_convert_fusion, bf16[2048,1]{1,0:T(8,128)(2,1)} %broadcast_in_dim.18, bf16[2048,1]{1,0:T(8,128)(2,1)S(1)} %copy-done.24, bf16[2048,1]{1,0:T(8,128)(2,1)S(1)} %copy-done.25), dimensions={1} | concatenate | bytes 159408128 | tf_op jit(solution)/shard_map/concatenate | solution.py:83
  1092.8 743.0 %reduce-scatter.3.cloned.1.call-done = bf16[128,19459]{1,0:T(8,128)(2,1)} async-done(((bf16[2048,19459]{1,0:T(8,128)(2,1)}), bf16[128,19459]{1,0:T(8,128)(2,1)}) %reduce-scatter.3.cloned.1.call-update) | async-done | bytes 4981520 | tf_op jit(solution)/shard_map/reduce_scatter | solution.py:202
  1835.9 2.9 fusion.28
  1838.7 12.3 fusion.8
  1851.0 143.4 %all-reduce.33.cloned.1.call-done = (bf16[128,19459]{1,0:T(8,128)(2,1)}, bf16[352,2048]{1,0:T(8,128)(2,1)}) async-done(((bf16[128,19459]{1,0:T(8,128)(2,1)}, bf16[352,2048]{1,0:T(8,128)(2,1)}), (bf16[128,19459]{1,0:T(8,128)(2,1)}, bf16[352,2048]{1,0:T(8,128)(2,1)})) %all-reduce.33.cloned.1.call-update) | async-done | bytes 6423312 | tf_op jit(solution)/shard_map/psum | solution.py:209
  1994.4 3.8 fusion.60
  1998.3 3.2 fusion.59
  (310 shorter events, 85.3 us)
Async XLA Ops:
  7.2 80.7 %all-gather.11.cloned.1.call-start = ((), (), s32[]{:S(2)}) async-start(), calls=%async_computation.2 | async-start | bytes 8912896 | tf_op jit(solution)/shard_map/all_gather | solution.py:113
  7.9 155.3 %all-gather.13.cloned.1.call-start = ((), (), s32[]{:S(2)}) async-start(), calls=%async_computation.3 | async-start | bytes 8912896 | tf_op jit(solution)/shard_map/all_gather | solution.py:114
  8.7 229.9 %all-gather.15.cloned.1.call-start = ((), (), s32[]{:S(2)}) async-start(), calls=%async_computation.4 | async-start | bytes 8912896 | tf_op jit(solution)/shard_map/all_gather | solution.py:115
  9.4 304.4 %all-gather.17.cloned.1.call-start = ((), (), s32[]{:S(2)}) async-start(), calls=%async_computation.5 | async-start | bytes 8912896 | tf_op jit(solution)/shard_map/all_gather | solution.py:132
  10.0 422.3 %all-gather.21.cloned.1.call-start = ((), (), s32[]{:S(2)}) async-start(), calls=%async_computation.7 | async-start | bytes 24510464 | tf_op jit(solution)/shard_map/all_gather | solution.py:143
  10.6 24.7 %copy-start.46 = (bf16[128]{0:T(256)(128)(2,1)S(1)}, bf16[128]{0:T(256)(128)(2,1)}, u32[]{:S(2)}) copy-start(bf16[128]{0:T(256)(128)(2,1)} %param.19) | copy-start | bytes 772
  10.6 42.1 %copy-start.47 = (bf16[128]{0:T(256)(128)(2,1)S(1)}, bf16[128]{0:T(256)(128)(2,1)}, u32[]{:S(2)}) copy-start(bf16[128]{0:T(256)(128)(2,1)} %param.21) | copy-start | bytes 772
  10.6 61.6 %copy-start.44 = (s32[1,192]{1,0:T(1,128)S(1)}, s32[1,192]{1,0:T(1,128)}, u32[]{:S(2)}) copy-start(s32[1,192]{1,0:T(1,128)} %param.14) | copy-start | bytes 2308
  10.6 61.8 %copy-start.1 = (bf16[1,192,2048]{2,1,0:T(8,128)(2,1)S(1)}, bf16[1,192,2048]{2,1,0:T(8,128)(2,1)}, u32[]{:S(2)}) copy-start(bf16[1,192,2048]{2,1,0:T(8,128)(2,1)} %param.13) | copy-start | bytes 2359300
  10.6 541.8 %all-gather.19.cloned.1.call-start = ((), (), s32[]{:S(2)}) async-start(), calls=%async_computation.6 | async-start | bytes 24510464 | tf_op jit(solution)/shard_map/all_gather | solution.py:142
  11.2 661.6 %all-gather.23.cloned.1.call-start = ((), (), s32[]{:S(2)}) async-start(), calls=%async_computation.8 | async-start | bytes 24510464 | tf_op jit(solution)/shard_map/all_gather | solution.py:152
  11.9 1080.8 %reduce-scatter.5.cloned.1.call-start = ((), (), s32[]{:S(2)}) async-start(), calls=%async_computation.10 | async-start | bytes 24510464 | tf_op jit(solution)/shard_map/reduce_scatter | solution.py:205
  72.4 90.9 %copy-start.42 = (f32[192]{0:T(256)}, f32[192]{0:T(256)S(1)}, u32[]{:S(2)}) copy-start(f32[192]{0:T(256)S(1)} %add_convert_fusion) | copy-start | bytes 2308
  72.6 90.6 %copy-start.32 = (f32[192]{0:T(256)}, f32[192]{0:T(256)S(1)}, u32[]{:S(2)}) copy-start(f32[192]{0:T(256)S(1)} %add_rsqrt_fusion.2) | copy-start | bytes 2308
  171.0 2.6 copy-start.3
  175.9 6.0 copy-start.10
  181.9 4.3 copy-start.13
  194.1 1.6 copy-start.18
  199.1 39.5 %copy-start.33 = (f32[192]{0:T(256)S(1)}, f32[192]{0:T(256)}, u32[]{:S(2)}) copy-start(f32[192]{0:T(256)} %copy-done.32) | copy-start | bytes 2308
  313.8 7.1 copy-start.31
  672.8 17.3 copy-start.20
  701.1 1134.7 %reduce-scatter.3.cloned.1.call-start = ((), (), s32[]{:S(2)}) async-start(), calls=%async_computation.9 | async-start | bytes 85229568 | tf_op jit(solution)/shard_map/reduce_scatter | solution.py:202
  743.2 2.2 copy-start.23
  745.4 12.2 copy-start.6
  772.0 2.2 copy-start.4
  772.0 2.7 copy-start.21
  772.0 3.2 copy-start.27
  791.4 8.7 copy-start.15
  810.3 3.6 copy-start.26
  819.0 5.8 copy-start.14
  822.9 7.7 copy-start.41
  832.9 1.7 copy-start.19
  846.6 16.0 copy-start.43
  862.6 11.0 slice-start
  866.8 6.9 copy-start.12
  866.8 6.9 slice-start.1
  866.8 9.8 slice-start.2
  873.7 2.9 copy-start.2
  873.7 2.9 slice-start.3
  873.7 2.9 copy-start.11
  873.7 2.9 copy-start.34
  876.6 5.4 copy-start.22
  913.7 20.9 %copy-start.24 = (bf16[2048,1]{1,0:T(8,128)(2,1)S(1)}, bf16[2048,1]{1,0:T(8,128)(2,1)}, u32[]{:S(2)}) copy-start(bf16[2048,1]{1,0:T(8,128)(2,1)} %broadcast_in_dim.19) | copy-start | bytes 12292
  913.7 20.9 %copy-start.25 = (bf16[2048,1]{1,0:T(8,128)(2,1)S(1)}, bf16[2048,1]{1,0:T(8,128)(2,1)}, u32[]{:S(2)}) copy-start(bf16[2048,1]{1,0:T(8,128)(2,1)} %broadcast_in_dim.20) | copy-start | bytes 12292
  1092.7 901.7 %all-reduce.33.cloned.1.call-start = ((), (), s32[]{:S(2)}) async-start(), calls=%async_computation.11 | async-start | bytes 12910592 | tf_op jit(solution)/shard_map/psum | solution.py:209
  1835.8 2.9 copy-start.7
  1835.9 2.9 copy-start.9
  1994.4 3.9 copy-start
  (14 other events, 14.5 us)
Sparse Core Ops, SparseCore 0:
  10.2 77.6 all-gather.10
  90.1 73.1 all-gather.12
  165.4 73.1 all-gather.14
  240.6 73.1 all-gather.16
  315.3 116.9 all-gather.20
  433.7 118.6 all-gather.18
  554.0 118.6 all-gather.22
  701.2 226.8 reduce-scatter.4
  1092.8 742.9 reduce-scatter.2
  1838.2 156.2 all-reduce.32
where the time goes:
time: 2030 us; the launch traced here: 2010 us
  waiting for transfers between devices  1400 us (69%)
  local copies, waits for them, and re-layouts  319 us (16%)
  matrix products  185 us (9%)
  blocking collectives  59.6 us (3%)
  other arithmetic  30.4 us (1%)
    reduce_scatter x1, waiting for transfers between devices, shards(): lax.psum_scatter(row_block(pairs, gains).astype(jnp.bfloat16), 'shard', s...  743 us
    concatenate x1, local copies, waits for them, and re-layouts, row_block(): return jnp.concatenate(pieces, axis=1)  158 us
    psum x1, waiting for transfers between devices, shards(): lax.psum(rows_term, 'rep').astype(jnp.float32)  143 us
    all_gather x1, waiting for transfers between devices, shards(): lax.all_gather(ffn_up_weight, 'shard', axis=0, tiled=True)  110 us
    all_gather x1, waiting for transfers between devices, shards(): lax.all_gather(ffn_gate_weight, 'shard', axis=0, tiled=True)  106 us
    all_gather x1, waiting for transfers between devices, shards(): lax.all_gather(ffn_down_weight, 'shard', axis=0, tiled=True)  106 us
    slice x90, local copies, waits for them, and re-layouts, linear_scan(): return lax.associative_scan(combine_steps, (decay, update), axis=0)[1]  96.4 us
    all_gather x1, waiting for transfers between devices, shards(): lax.all_gather(forget_weight, 'shard', axis=0, tiled=True)  69 us
  transfers between devices with their start and end apart: 10, of which 9 were waited for; matrix products, arithmetic and copies ran while one was open for 24% of the time, Pallas kernels for 0%

commit v1 on v0

--- a/solution.py
+++ b/solution.py
@@ -4,6 +4,28 @@
 from jax.sharding import PartitionSpec as P
 
 EPSILON = 1e-06
+
+
+def in_order(blocks, dim):
+    shape = list(blocks.shape[1:])
+    shape[dim] *= blocks.shape[0]
+    return jnp.moveaxis(blocks, 0, dim).reshape(shape)
+
+
+def ring_gather(x, axis, dim):
+    peers = lax.axis_size(axis)
+    pairs = [(i, (i + 1) % peers) for i in range(peers)]
+    back = [(b, a) for a, b in pairs]
+    lower, upper = ([], [])
+    for step in range(peers - 1):
+        if step % 2 == 0:
+            lower.append(lax.ppermute(lower[-1] if lower else x, axis, pairs))
+        else:
+            upper.append(lax.ppermute(upper[-1] if upper else x, axis, back))
+    blocks = jnp.stack([*lower[::-1], x, *upper])
+    shift = lax.axis_index(axis) - len(lower)
+    blocks = blocks[(jnp.arange(peers) - shift) % peers]
+    return in_order(blocks, dim)
 
 
 def normalize(values):
@@ -140,7 +162,7 @@
         start_carry(length, width, hidden_width, 2),
         (
             lax.all_gather(ffn_gate_weight, "shard", axis=0, tiled=True),
-            lax.all_gather(ffn_up_weight, "shard", axis=0, tiled=True),
+            ring_gather(ffn_up_weight, "shard", 0),
             lax.all_gather(ffn_gain, "shard", axis=0, tiled=True),
         ),
     )

time: 2030 us -> 2140 us (1.054)
  waiting for transfers between devices: 1400 us -> 1230 us
  local copies, waits for them, and re-layouts: 319 us -> 466 us
  starting transfers between devices: 0.39 us -> 88.5 us
  other arithmetic: 30.4 us -> 53.5 us
    ppermute x0 -> x15, waiting for transfers between devices: none -> 189 us  [the longest x8 188 us: ring_gather(): lower.append(lax.ppermute(lower[-1] if lower else x, axis, pairs))]
    slice x90, local copies, waits for them, and re-layouts: 96.4 us -> 194 us  [linear_scan(): return lax.associative_scan(combine_steps, (decay, update), axis=0)[1]]
    ppermute x0 -> x15, starting transfers between devices: none -> 88.1 us  [the longest x8 77.2 us: ring_gather(): lower.append(lax.ppermute(lower[-1] if lower else x, axis, pairs))]
    all_gather x1, waiting for transfers between devices: 110 us -> 24.3 us  [shards(): lax.all_gather((ffn_gate_weight, ffn_up_weight), 'shard', axis=0, tiled=T...]
    all_gather x1, waiting for transfers between devices: 106 us -> 24.4 us  [shards(): lax.all_gather(ffn_down_weight, 'shard', axis=0, tiled=True)]
    all_gather x1, waiting for transfers between devices: 69 us -> 0.01 us  [shards(): lax.all_gather(forget_weight, 'shard', axis=0, tiled=True)]
    all_gather x1, waiting for transfers between devices: 67.6 us -> 0.01 us  [shards(): lax.all_gather(out_weight, 'shard', axis=0, tiled=True)]
    all_gather x1, waiting for transfers between devices: 38.1 us -> 0.01 us  [shards(): lax.all_gather(gate_weight, 'shard', axis=0, tiled=True)]
  transfers between devices with their start and end apart: 10 -> 25, of which waited for: 9 -> 13; matrix products, arithmetic and copies ran while one was open for 24% -> 32% of each run, Pallas kernels for 0% -> 0%
where the time goes in v1:
time: 2140 us; the launch traced here: 2120 us
  waiting for transfers between devices  1230 us (57%)
  local copies, waits for them, and re-layouts  466 us (22%)
  matrix products  184 us (9%)
  starting transfers between devices  88.5 us (4%)
  blocking collectives  80.3 us (4%)
  other arithmetic  53.5 us (2%)
    reduce_scatter x1, waiting for transfers between devices, shards(): lax.psum_scatter(row_block(pairs, gains).astype(jnp.bfloat16), 'shard', s...  743 us
    slice x90, local copies, waits for them, and re-layouts, linear_scan(): return lax.associative_scan(combine_steps, (decay, update), axis=0)[1]  194 us
    ppermute x8, waiting for transfers between devices, ring_gather(): lower.append(lax.ppermute(lower[-1] if lower else x, axis, pairs))  188 us
    concatenate x1, local copies, waits for them, and re-layouts, row_block(): return jnp.concatenate(pieces, axis=1)  158 us
    psum x1, waiting for transfers between devices, shards(): lax.psum(rows_term, 'rep').astype(jnp.float32)  143 us
    all_gather x1, waiting for transfers between devices, shards(): lax.all_gather(ffn_gate_weight, 'shard', axis=0, tiled=True)  107 us
    ppermute x8, starting transfers between devices, ring_gather(): lower.append(lax.ppermute(lower[-1] if lower else x, axis, pairs))  77.2 us
    dot_general x7, matrix products, contract_rows(): lax.dot_general(left, piece, (((1,), (1,)), ((), ())), preferred_element_...  64.6 us
  transfers between devices with their start and end apart: 25, of which 13 were waited for; matrix products, arithmetic and copies ran while one was open for 32% of the time, Pallas kernels for 0%

profile of v1, /device:TPU:0, one launch (start us, length us, event | category | flops | bytes accessed | tf_op | source)
XLA Modules:
  0.0 2122.1 jit_solution(1491676523445934297)
XLA Ops:
  11.8 35.1 %collective-permute-done = bf16[128,5632]{1,0:T(8,128)(2,1)S(1)} collective-permute-done((bf16[128,5632]{1,0:T(8,128)(2,1)S(1)}, bf16[128,5632]{1,0:T(8,128)(2,1)S(1)}, u32[]{:S(2)}, u32[]{:S(2)}) %collective-permute-start) | collective-permute-done | bytes 1441824 | tf_op jit(solution)/shard_map/ppermute | solution.py:22
  51.3 34.5 %collective-permute-done.1 = bf16[128,5632]{1,0:T(8,128)(2,1)S(1)} collective-permute-done((bf16[128,5632]{1,0:T(8,128)(2,1)S(1)}, bf16[128,5632]{1,0:T(8,128)(2,1)S(1)}, u32[]{:S(2)}, u32[]{:S(2)}) %collective-permute-start.1) | collective-permute-done | bytes 1441824 | tf_op jit(solution)/shard_map/ppermute | solution.py:22
  90.3 16.7 collective-permute-done.2
  107.1 16.2 collective-permute-start.3
  123.3 25.2 %collective-permute-done.3 = bf16[128,5632]{1,0:T(8,128)(2,1)S(1)} collective-permute-done((bf16[128,5632]{1,0:T(8,128)(2,1)S(1)}, bf16[128,5632]{1,0:T(8,128)(2,1)S(1)}, u32[]{:S(2)}, u32[]{:S(2)}) %collective-permute-start.3) | collective-permute-done | bytes 1441824 | tf_op jit(solution)/shard_map/ppermute | solution.py:22
  148.5 8.4 collective-permute-start.4
  158.0 24.6 %collective-permute-done.4 = bf16[128,5632]{1,0:T(8,128)(2,1)S(1)} collective-permute-done((bf16[128,5632]{1,0:T(8,128)(2,1)S(1)}, bf16[128,5632]{1,0:T(8,128)(2,1)S(1)}, u32[]{:S(2)}, u32[]{:S(2)}) %collective-permute-start.4) | collective-permute-done | bytes 1441824 | tf_op jit(solution)/shard_map/ppermute | solution.py:22
  182.6 12.2 collective-permute-start.5
  196.2 28.1 %collective-permute-done.5 = bf16[128,5632]{1,0:T(8,128)(2,1)S(1)} collective-permute-done((bf16[128,5632]{1,0:T(8,128)(2,1)S(1)}, bf16[128,5632]{1,0:T(8,128)(2,1)S(1)}, u32[]{:S(2)}, u32[]{:S(2)}) %collective-permute-start.5) | collective-permute-done | bytes 1441824 | tf_op jit(solution)/shard_map/ppermute | solution.py:22
  224.3 25.5 %collective-permute-start.6 = (bf16[128,5632]{1,0:T(8,128)(2,1)S(1)}, bf16[128,5632]{1,0:T(8,128)(2,1)}, u32[]{:S(2)}, u32[]{:S(2)}) collective-permute-start(bf16[128,5632]{1,0:T(8,128)(2,1)S(1)} %collective-permute-done.5), channel_id=1, source_target_pairs={{0,1},{1,2},{2,3},{3,4},{4,5},{5,6},{6,7},{7,8},{8,9},{9,10},{10,1... | collective-permute-start | bytes 4325384 | tf_op jit(solution)/shard_map/ppermute | solution.py:22
  251.0 23.9 %collective-permute-done.6 = bf16[128,5632]{1,0:T(8,128)(2,1)} collective-permute-done((bf16[128,5632]{1,0:T(8,128)(2,1)S(1)}, bf16[128,5632]{1,0:T(8,128)(2,1)}, u32[]{:S(2)}, u32[]{:S(2)}) %collective-permute-start.6) | collective-permute-done | bytes 1441824 | tf_op jit(solution)/shard_map/ppermute | solution.py:22
  274.9 14.4 collective-permute-start.7
  289.8 42.9 %all-gather = bf16[16,1,128]{2,1,0:T(2,128)(2,1)S(1)} all-gather(bf16[1,1,128]{2,1,0:T(2,128)(2,1)S(1)} %bitcast.109), channel_id=1, replica_groups=mesh['rep'=2,'shard'=16] {'shard'}, dimensions={0}, use_global_device_ids=true | all-gather | bytes 4352 | tf_op jit(solution)/shard_map/all_gather | solution.py:138
  332.7 20.1 all-gather.1
  352.9 17.3 all-gather.2
  403.6 17.5 gather_fusion
  421.1 6.5 fusion.59
  427.6 8.1 broadcast_multiply_fusion
  442.4 4.6 slice.444
  522.9 7.8 multiply_multiply_fusion.1
  530.7 6.2 multiply_reduce_fusion.4
  539.1 24.4 %all-gather.21.cloned.1.call-done = bf16[5632,2048]{1,0:T(8,128)(2,1)} async-done(((bf16[352,2048]{1,0:T(8,128)(2,1)}), bf16[5632,2048]{1,0:T(8,128)(2,1)}) %all-gather.21.cloned.1.call-update) | async-done | bytes 23068688 | tf_op jit(solution)/shard_map/all_gather | solution.py:174
  563.5 13.6 fusion.32
  577.1 106.6 %all-gather.19.cloned.1.call-done = bf16[2048,5632]{1,0:T(8,128)(2,1)} async-done(((bf16[128,5632]{1,0:T(8,128)(2,1)}), bf16[2048,5632]{1,0:T(8,128)(2,1)}) %all-gather.19.cloned.1.call-update) | async-done | bytes 23068688 | tf_op jit(solution)/shard_map/all_gather | solution.py:164
  683.7 12.7 fusion.75
  696.4 14.5 multiply_convert_fusion
  712.2 11.2 convolution_convert_fusion.1
  739.4 8.6 slice.448
  748.0 8.5 slice.457
  756.5 8.6 slice.450
  767.3 12.4 fusion.76
  779.7 24.3 %all-gather.23.cloned.1.call-done = bf16[2048,5632]{1,0:T(8,128)(2,1)} async-done(((bf16[128,5632]{1,0:T(8,128)(2,1)}), bf16[2048,5632]{1,0:T(8,128)(2,1)}) %all-gather.23.cloned.1.call-update) | async-done | bytes 23068688 | tf_op jit(solution)/shard_map/all_gather | solution.py:185
  804.0 14.3 multiply_reduce_fusion
  823.1 10.4 multiply_reduce_fusion.1
  840.6 8.6 slice.454
  849.2 8.6 slice.452
  927.2 9.0 slice.504
  945.1 5.2 pad.115
  953.1 16.2 rev.6
  969.3 5.8 convolution_convert_fusion.3
  975.1 12.4 copy.30
  991.6 6.6 fusion.77
  1009.0 13.5 convolution_convert_fusion.2
  1022.6 21.0 convolution_convert_fusion
  1043.6 158.0 %concatenate.84 = bf16[2048,19459]{1,0:T(8,128)(2,1)} concatenate(bf16[2048,6144]{1,0:T(8,128)(2,1)} %convolution_convert_fusion.2, bf16[2048,2048]{1,0:T(8,128)(2,1)} %copy.30, bf16[2048,11264]{1,0:T(8,128)(2,1)} %convolution_convert_fusion, bf16[2048,1]{1,0:T(8,128)(2,1)S(1)} %copy-done.24, bf16[2048,1]{1,0:T(8,128)(2,1)S(1)} %copy-done.25, bf16[2048,1]{1,0:T(8,128)(2,1)} %broadcast_in_dim.20), dimensions={1} | concatenate | bytes 159408128 | tf_op jit(solution)/shard_map/concatenate | solution.py:105
  1201.7 742.8 %reduce-scatter.3.cloned.1.call-done = bf16[128,19459]{1,0:T(8,128)(2,1)} async-done(((bf16[2048,19459]{1,0:T(8,128)(2,1)}), bf16[128,19459]{1,0:T(8,128)(2,1)}) %reduce-scatter.3.cloned.1.call-update) | async-done | bytes 4981520 | tf_op jit(solution)/shard_map/reduce_scatter | solution.py:224
  1947.5 12.3 fusion.8
  1959.7 143.4 %all-reduce.33.cloned.1.call-done = (bf16[128,19459]{1,0:T(8,128)(2,1)}, bf16[352,2048]{1,0:T(8,128)(2,1)}) async-done(((bf16[128,19459]{1,0:T(8,128)(2,1)}, bf16[352,2048]{1,0:T(8,128)(2,1)}), (bf16[128,19459]{1,0:T(8,128)(2,1)}, bf16[352,2048]{1,0:T(8,128)(2,1)})) %all-reduce.33.cloned.1.call-update) | async-done | bytes 6423312 | tf_op jit(solution)/shard_map/psum | solution.py:231
  (433 shorter events, 277.3 us)
Async XLA Ops:
  7.2 413.9 %all-gather.11.cloned.1.call-start = ((), (), s32[]{:S(2)}) async-start(), calls=%async_computation.2 | async-start | bytes 8912896 | tf_op jit(solution)/shard_map/all_gather | solution.py:135
  7.9 419.7 %all-gather.13.cloned.1.call-start = ((), (), s32[]{:S(2)}) async-start(), calls=%async_computation.3 | async-start | bytes 8912896 | tf_op jit(solution)/shard_map/all_gather | solution.py:136
  8.7 514.2 %all-gather.15.cloned.1.call-start = ((), (), s32[]{:S(2)}) async-start(), calls=%async_computation.4 | async-start | bytes 8912896 | tf_op jit(solution)/shard_map/all_gather | solution.py:137
  9.4 521.3 %all-gather.17.cloned.1.call-start = ((), (), s32[]{:S(2)}) async-start(), calls=%async_computation.5 | async-start | bytes 8912896 | tf_op jit(solution)/shard_map/all_gather | solution.py:154
  10.0 553.5 %all-gather.21.cloned.1.call-start = ((), (), s32[]{:S(2)}) async-start(), calls=%async_computation.7 | async-start | bytes 24510464 | tf_op jit(solution)/shard_map/all_gather | solution.py:174
  10.6 278.8 %copy-start.81 = (s32[1,192]{1,0:T(1,128)S(1)}, s32[1,192]{1,0:T(1,128)}, u32[]{:S(2)}) copy-start(s32[1,192]{1,0:T(1,128)} %param.14) | copy-start | bytes 2308
  10.6 278.9 %copy-start.1 = (bf16[1,192,2048]{2,1,0:T(8,128)(2,1)S(1)}, bf16[1,192,2048]{2,1,0:T(8,128)(2,1)}, u32[]{:S(2)}) copy-start(bf16[1,192,2048]{2,1,0:T(8,128)(2,1)} %param.13) | copy-start | bytes 2359300
  10.6 279.2 %copy-start.82 = (bf16[128]{0:T(256)(128)(2,1)S(1)}, bf16[128]{0:T(256)(128)(2,1)}, u32[]{:S(2)}) copy-start(bf16[128]{0:T(256)(128)(2,1)} %param.15) | copy-start | bytes 772
  10.6 322.1 %copy-start.83 = (bf16[128]{0:T(256)(128)(2,1)S(1)}, bf16[128]{0:T(256)(128)(2,1)}, u32[]{:S(2)}) copy-start(bf16[128]{0:T(256)(128)(2,1)} %param.19) | copy-start | bytes 772
  10.6 342.3 %copy-start.84 = (bf16[128]{0:T(256)(128)(2,1)S(1)}, bf16[128]{0:T(256)(128)(2,1)}, u32[]{:S(2)}) copy-start(bf16[128]{0:T(256)(128)(2,1)} %param.21) | copy-start | bytes 772
  10.6 673.0 %all-gather.19.cloned.1.call-start = ((), (), s32[]{:S(2)}) async-start(), calls=%async_computation.6 | async-start | bytes 24510464 | tf_op jit(solution)/shard_map/all_gather | solution.py:164
  11.2 792.8 %all-gather.23.cloned.1.call-start = ((), (), s32[]{:S(2)}) async-start(), calls=%async_computation.8 | async-start | bytes 24510464 | tf_op jit(solution)/shard_map/all_gather | solution.py:185
  11.3 35.6 %collective-permute-start = (bf16[128,5632]{1,0:T(8,128)(2,1)S(1)}, bf16[128,5632]{1,0:T(8,128)(2,1)S(1)}, u32[]{:S(2)}, u32[]{:S(2)}) collective-permute-start(bf16[128,5632]{1,0:T(8,128)(2,1)S(1)} %copy-done.8), channel_id=1, source_target_pairs={{0,1},{1,2},{2,3},{3,4},{4,5},{5,6},{6,7},{7,8},{8,9},{9,10},{10,1... | collective-permute-start | bytes 4325384 | tf_op jit(solution)/shard_map/ppermute | solution.py:22
  46.8 39.0 %copy-start.28 = (bf16[128,5632]{1,0:T(8,128)(2,1)}, bf16[128,5632]{1,0:T(8,128)(2,1)S(1)}, u32[]{:S(2)}) copy-start(bf16[128,5632]{1,0:T(8,128)(2,1)S(1)} %collective-permute-done) | copy-start | bytes 4325380
  46.8 39.0 %collective-permute-start.1 = (bf16[128,5632]{1,0:T(8,128)(2,1)S(1)}, bf16[128,5632]{1,0:T(8,128)(2,1)S(1)}, u32[]{:S(2)}, u32[]{:S(2)}) collective-permute-start(bf16[128,5632]{1,0:T(8,128)(2,1)S(1)} %collective-permute-done), channel_id=1, source_target_pairs={{0,1},{1,2},{2,3},{3,4},{4,5},{5,6},{6,7},{7,8},{8,9},{9,10},{10,1... | collective-permute-start | bytes 4325384 | tf_op jit(solution)/shard_map/ppermute | solution.py:22
  46.8 39.0 %collective-permute-start.8 = (bf16[128,5632]{1,0:T(8,128)(2,1)S(1)}, bf16[128,5632]{1,0:T(8,128)(2,1)S(1)}, u32[]{:S(2)}, u32[]{:S(2)}) collective-permute-start(bf16[128,5632]{1,0:T(8,128)(2,1)S(1)} %copy-done.8), channel_id=1, source_target_pairs={{1,0},{2,1},{3,2},{4,3},{5,4},{6,5},{7,6},{8,7},{9,8},{10,9},{11,1... | collective-permute-start | bytes 4325384 | tf_op jit(solution)/shard_map/ppermute | solution.py:24
  85.8 37.4 %copy-start.32 = (bf16[128,5632]{1,0:T(8,128)(2,1)}, bf16[128,5632]{1,0:T(8,128)(2,1)S(1)}, u32[]{:S(2)}) copy-start(bf16[128,5632]{1,0:T(8,128)(2,1)S(1)} %collective-permute-done.1) | copy-start | bytes 4325380
  85.8 21.2 %collective-permute-start.2 = (bf16[128,5632]{1,0:T(8,128)(2,1)S(1)}, bf16[128,5632]{1,0:T(8,128)(2,1)S(1)}, u32[]{:S(2)}, u32[]{:S(2)}) collective-permute-start(bf16[128,5632]{1,0:T(8,128)(2,1)S(1)} %collective-permute-done.1), channel_id=1, source_target_pairs={{0,1},{1,2},{2,3},{3,4},{4,5},{5,6},{6,7},{7,8},{8,9},{9,10},{10,1... | collective-permute-start | bytes 4325384 | tf_op jit(solution)/shard_map/ppermute | solution.py:22
  85.8 37.4 %collective-permute-start.9 = (bf16[128,5632]{1,0:T(8,128)(2,1)S(1)}, bf16[128,5632]{1,0:T(8,128)(2,1)S(1)}, u32[]{:S(2)}, u32[]{:S(2)}) collective-permute-start(bf16[128,5632]{1,0:T(8,128)(2,1)S(1)} %collective-permute-done.8), channel_id=1, source_target_pairs={{1,0},{2,1},{3,2},{4,3},{5,4},{6,5},{7,6},{8,7},{9,8},{10,9},{11,1... | collective-permute-start | bytes 4325384 | tf_op jit(solution)/shard_map/ppermute | solution.py:24
  107.1 49.9 %copy-start.34 = (bf16[128,5632]{1,0:T(8,128)(2,1)}, bf16[128,5632]{1,0:T(8,128)(2,1)S(1)}, u32[]{:S(2)}) copy-start(bf16[128,5632]{1,0:T(8,128)(2,1)S(1)} %collective-permute-done.2) | copy-start | bytes 4325380
  107.1 41.5 %collective-permute-start.3 = (bf16[128,5632]{1,0:T(8,128)(2,1)S(1)}, bf16[128,5632]{1,0:T(8,128)(2,1)S(1)}, u32[]{:S(2)}, u32[]{:S(2)}) collective-permute-start(bf16[128,5632]{1,0:T(8,128)(2,1)S(1)} %collective-permute-done.2), channel_id=1, source_target_pairs={{0,1},{1,2},{2,3},{3,4},{4,5},{5,6},{6,7},{7,8},{8,9},{9,10},{10,1... | collective-permute-start | bytes 4325384 | tf_op jit(solution)/shard_map/ppermute | solution.py:22
  123.2 33.7 %collective-permute-start.10 = (bf16[128,5632]{1,0:T(8,128)(2,1)S(1)}, bf16[128,5632]{1,0:T(8,128)(2,1)S(1)}, u32[]{:S(2)}, u32[]{:S(2)}) collective-permute-start(bf16[128,5632]{1,0:T(8,128)(2,1)S(1)} %collective-permute-done.9), channel_id=1, source_target_pairs={{1,0},{2,1},{3,2},{4,3},{5,4},{6,5},{7,6},{8,7},{9,8},{10,9},{11,1... | collective-permute-start | bytes 4325384 | tf_op jit(solution)/shard_map/ppermute | solution.py:24
  148.5 102.5 %copy-start.40 = (bf16[128,5632]{1,0:T(8,128)(2,1)}, bf16[128,5632]{1,0:T(8,128)(2,1)S(1)}, u32[]{:S(2)}) copy-start(bf16[128,5632]{1,0:T(8,128)(2,1)S(1)} %collective-permute-done.3) | copy-start | bytes 4325380
  148.5 34.1 %collective-permute-start.4 = (bf16[128,5632]{1,0:T(8,128)(2,1)S(1)}, bf16[128,5632]{1,0:T(8,128)(2,1)S(1)}, u32[]{:S(2)}, u32[]{:S(2)}) collective-permute-start(bf16[128,5632]{1,0:T(8,128)(2,1)S(1)} %collective-permute-done.3), channel_id=1, source_target_pairs={{0,1},{1,2},{2,3},{3,4},{4,5},{5,6},{6,7},{7,8},{8,9},{9,10},{10,1... | collective-permute-start | bytes 4325384 | tf_op jit(solution)/shard_map/ppermute | solution.py:22
  156.9 37.9 %collective-permute-start.11 = (bf16[128,5632]{1,0:T(8,128)(2,1)S(1)}, bf16[128,5632]{1,0:T(8,128)(2,1)S(1)}, u32[]{:S(2)}, u32[]{:S(2)}) collective-permute-start(bf16[128,5632]{1,0:T(8,128)(2,1)S(1)} %collective-permute-done.10), channel_id=1, source_target_pairs={{1,0},{2,1},{3,2},{4,3},{5,4},{6,5},{7,6},{8,7},{9,8},{10,9},{11,1... | collective-permute-start | bytes 4325384 | tf_op jit(solution)/shard_map/ppermute | solution.py:24
  182.6 68.4 %copy-start.42 = (bf16[128,5632]{1,0:T(8,128)(2,1)}, bf16[128,5632]{1,0:T(8,128)(2,1)S(1)}, u32[]{:S(2)}) copy-start(bf16[128,5632]{1,0:T(8,128)(2,1)S(1)} %collective-permute-done.4) | copy-start | bytes 4325380
  182.6 41.6 %collective-permute-start.5 = (bf16[128,5632]{1,0:T(8,128)(2,1)S(1)}, bf16[128,5632]{1,0:T(8,128)(2,1)S(1)}, u32[]{:S(2)}, u32[]{:S(2)}) collective-permute-start(bf16[128,5632]{1,0:T(8,128)(2,1)S(1)} %collective-permute-done.4), channel_id=1, source_target_pairs={{0,1},{1,2},{2,3},{3,4},{4,5},{5,6},{6,7},{7,8},{8,9},{9,10},{10,1... | collective-permute-start | bytes 4325384 | tf_op jit(solution)/shard_map/ppermute | solution.py:22
  195.9 55.1 %collective-permute-start.12 = (bf16[128,5632]{1,0:T(8,128)(2,1)S(1)}, bf16[128,5632]{1,0:T(8,128)(2,1)}, u32[]{:S(2)}, u32[]{:S(2)}) collective-permute-start(bf16[128,5632]{1,0:T(8,128)(2,1)S(1)} %collective-permute-done.11), channel_id=1, source_target_pairs={{1,0},{2,1},{3,2},{4,3},{5,4},{6,5},{7,6},{8,7},{9,8},{10,9},{11,1... | collective-permute-start | bytes 4325384 | tf_op jit(solution)/shard_map/ppermute | solution.py:24
  224.3 50.7 %copy-start.44 = (bf16[128,5632]{1,0:T(8,128)(2,1)}, bf16[128,5632]{1,0:T(8,128)(2,1)S(1)}, u32[]{:S(2)}) copy-start(bf16[128,5632]{1,0:T(8,128)(2,1)S(1)} %collective-permute-done.5) | copy-start | bytes 4325380
  224.3 50.7 %collective-permute-start.6 = (bf16[128,5632]{1,0:T(8,128)(2,1)S(1)}, bf16[128,5632]{1,0:T(8,128)(2,1)}, u32[]{:S(2)}, u32[]{:S(2)}) collective-permute-start(bf16[128,5632]{1,0:T(8,128)(2,1)S(1)} %collective-permute-done.5), channel_id=1, source_target_pairs={{0,1},{1,2},{2,3},{3,4},{4,5},{5,6},{6,7},{7,8},{8,9},{9,10},{10,1... | collective-permute-start | bytes 4325384 | tf_op jit(solution)/shard_map/ppermute | solution.py:22
  251.0 119.8 %collective-permute-start.13 = (bf16[128,5632]{1,0:T(8,128)(2,1)}, bf16[128,5632]{1,0:T(8,128)(2,1)}, u32[]{:S(2)}, u32[]{:S(2)}) collective-permute-start(bf16[128,5632]{1,0:T(8,128)(2,1)} %collective-permute-done.12), channel_id=1, source_target_pairs={{1,0},{2,1},{3,2},{4,3},{5,4},{6,5},{7,6},{8,7},{9,8},{10,9},{11,1... | collective-permute-start | bytes 4325384 | tf_op jit(solution)/shard_map/ppermute | solution.py:24
  274.9 97.5 %collective-permute-start.7 = (bf16[128,5632]{1,0:T(8,128)(2,1)}, bf16[128,5632]{1,0:T(8,128)(2,1)}, u32[]{:S(2)}, u32[]{:S(2)}) collective-permute-start(bf16[128,5632]{1,0:T(8,128)(2,1)} %collective-permute-done.6), channel_id=1, source_target_pairs={{0,1},{1,2},{2,3},{3,4},{4,5},{5,6},{6,7},{7,8},{8,9},{9,10},{10,1... | collective-permute-start | bytes 4325384 | tf_op jit(solution)/shard_map/ppermute | solution.py:22
  289.3 912.4 %reduce-scatter.5.cloned.1.call-start = ((), (), s32[]{:S(2)}) async-start(), calls=%async_computation.10 | async-start | bytes 24510464 | tf_op jit(solution)/shard_map/reduce_scatter | solution.py:227
  289.8 137.8 %copy-start.64 = (f32[192]{0:T(256)}, f32[192]{0:T(256)S(1)}, u32[]{:S(2)}) copy-start(f32[192]{0:T(256)S(1)} %add_rsqrt_fusion.2) | copy-start | bytes 2308
  289.8 137.7 %copy-start.79 = (f32[192]{0:T(256)}, f32[192]{0:T(256)S(1)}, u32[]{:S(2)}) copy-start(f32[192]{0:T(256)S(1)} %add_convert_fusion) | copy-start | bytes 2308
  370.8 31.5 %collective-permute-start.14 = (bf16[128,5632]{1,0:T(8,128)(2,1)}, bf16[128,5632]{1,0:T(8,128)(2,1)S(1)}, u32[]{:S(2)}, u32[]{:S(2)}) collective-permute-start(bf16[128,5632]{1,0:T(8,128)(2,1)} %collective-permute-done.13), channel_id=1, source_target_pairs={{1,0},{2,1},{3,2},{4,3},{5,4},{6,5},{7,6},{8,7},{9,8},{10,9},{11,1... | collective-permute-start | bytes 4325384 | tf_op jit(solution)/shard_map/ppermute | solution.py:24
  696.4 15.8 copy-start.19
  723.4 1221.1 %reduce-scatter.3.cloned.1.call-start = ((), (), s32[]{:S(2)}) async-start(), calls=%async_computation.9 | async-start | bytes 85229568 | tf_op jit(solution)/shard_map/reduce_scatter | solution.py:224
  767.3 36.7 %copy-start.6 = (f32[192,2048]{1,0:T(8,128)S(1)}, f32[192,2048]{1,0:T(8,128)}, u32[]{:S(2)}) copy-start(f32[192,2048]{1,0:T(8,128)} %copy-done.5) | copy-start | bytes 4718596
  919.4 16.7 copy-start.57
  919.4 16.7 copy-start.58
  919.5 16.7 copy-start.59
  919.5 16.8 copy-start.60
  922.3 14.3 copy-start.56
  953.1 16.2 copy-start.22
  1022.6 21.0 copy-start.24
  1022.6 21.0 copy-start.25
  1201.6 901.5 %all-reduce.33.cloned.1.call-start = ((), (), s32[]{:S(2)}) async-start(), calls=%async_computation.11 | async-start | bytes 12910592 | tf_op jit(solution)/shard_map/psum | solution.py:231
  (66 other events, 262.2 us)
Sparse Core Ops, SparseCore 0:
  10.2 125.7 all-gather.10
  138.2 119.7 all-gather.12
  260.2 96.5 all-gather.14
  358.8 86.2 all-gather.16
  446.5 116.9 all-gather.20
  564.9 118.6 all-gather.18
  685.3 118.6 all-gather.22
  808.1 226.6 reduce-scatter.4
  1201.8 742.7 reduce-scatter.2
  1946.9 156.2 all-reduce.32
